TPU v7x, 256 devices: a whole 4x4x8 slice. The times are simulated.
256 devices in a mesh: grp: 8 (over z_lo, core), slab: 32 (over z_hi, x, y).
Axes of the slice: x: 4, y: 4, z: 8 (z_hi: 2, z_lo: 4; z = z_hi * 4 + z_lo), core: 2. Of those that a mesh axis runs over, the one named last changes fastest.
Arguments:
- occ_orbitals: bfloat16 [1024, 64, 4096], P(('grp', 'slab')), may hold values from -6 to 6
- vir_orbitals: bfloat16 [2048, 64, 4096], P(('grp', 'slab')), may hold values from -6 to 6
- pair_occ: int32 [8192], P(('grp', 'slab')), may hold values from 0 to 3
- pair_vir: int32 [8192], P(('grp', 'slab')), may hold values from 0 to 7
- sketch: bfloat16 [8192, 1024], P('grp'), may hold values from -6 to 6
Outputs:
- vertex: float32 [8192, 1024], P(('grp', 'slab'))
Inputs may be any that keep to these rules, and one draw needn't show every extreme that they name: `pair_occ`: an index into the 4 occupied orbitals held by the same device as the pair. `pair_vir`: an index into the 8 virtual orbitals held by the same device as the pair.
All inputs are finite; a program needn't handle non-finite values.
Results may differ from a plain program's by a relative error of at most 0.0057.
Values may be sent and summed in bfloat16 or wider, within the bound.
No kernel may reach another device: no remote copies, remote signals or barrier semaphores. Data moves between devices by JAX's collectives and lax.ppermute only.
A program may use at most 192 MiB of HBM per device.

v0:
```python
import math
import jax
import jax.numpy as jnp
from jax import lax
from jax.sharding import PartitionSpec as P

KYZ = 32
box_length = 10.0
screening = 1.0
epsilon = 1e-06


def real_basis(points, mode_count):
    grid_cells = jnp.arange(points, dtype=jnp.float32)[:, None]
    mode_index = jnp.arange(mode_count, dtype=jnp.int32)[None, :]
    frequency = (mode_index + 1) // 2
    phases = 2.0 * math.pi * grid_cells * frequency.astype(jnp.float32) / points
    values = jnp.where((mode_index % 2 == 1) | (mode_index == 0), jnp.cos(phases), jnp.sin(phases))
    factor = jnp.where(
        (mode_index == 0) | (2 * frequency == points),
        math.sqrt(1.0 / points),
        math.sqrt(2.0 / points),
    )
    return (values * factor).astype(jnp.bfloat16)


def coulomb_weight(modes_x, plane_count):
    freq_x = ((jnp.arange(modes_x, dtype=jnp.int32) + 1) // 2).astype(jnp.float32)
    freq_p = ((jnp.arange(plane_count, dtype=jnp.int32) + 1) // 2).astype(jnp.float32)
    plane_sq = (freq_p[:, None] * freq_p[:, None] + freq_p[None, :] * freq_p[None, :]).reshape(-1)
    summed_sq = plane_sq[:, None, None] + (freq_x * freq_x)[None, None, :]
    wave_sq = (2.0 * math.pi / box_length) ** 2 * summed_sq
    return jnp.sqrt(4.0 * math.pi / (wave_sq + screening * screening))


def pair_coefficients(occ_rows, vir_rows):
    pairs_dev = occ_rows.shape[0]
    grid_size = occ_rows.shape[1]
    basis_x = real_basis(grid_size, grid_size)
    basis_plane = real_basis(grid_size, KYZ)
    density = (occ_rows.astype(jnp.float32) * vir_rows.astype(jnp.float32)).astype(jnp.bfloat16)
    along_x = jnp.einsum(
        "pxs,xk->pks", density, basis_x, preferred_element_type=jnp.float32
    ).astype(jnp.bfloat16)
    planes = along_x.reshape(pairs_dev * grid_size, grid_size, grid_size)
    second = jnp.einsum(
        "ayz,zc->cya", planes, basis_plane, preferred_element_type=jnp.float32
    ).astype(jnp.bfloat16)
    along_y = jnp.einsum("cya,yb->bca", second, basis_plane, preferred_element_type=jnp.float32)
    weighted = along_y.reshape(KYZ * KYZ, pairs_dev, grid_size) * coulomb_weight(grid_size, KYZ)
    return weighted.astype(jnp.bfloat16)


def body(occ_orbitals, vir_orbitals, pair_occ, pair_vir, sketch):
    coulomb_rows = pair_coefficients(occ_orbitals[pair_occ], vir_orbitals[pair_vir])
    plane_modes, pairs_dev, modes_x = coulomb_rows.shape
    slab_count = lax.axis_size("slab")
    fields = sketch.shape[1]
    parcel = coulomb_rows.reshape(slab_count, plane_modes // slab_count, pairs_dev * modes_x)
    received = lax.all_to_all(parcel, "slab", split_axis=0, concat_axis=2, tiled=True)
    item_count = received.shape[1]
    grouped = received[0].reshape(item_count, -1, modes_x)
    partial_value = jnp.einsum("npk,pf->nkf", grouped, sketch, preferred_element_type=jnp.float32)
    partial_value, local_rows = (partial_value, received[0])
    flattened = partial_value.reshape(-1, fields)
    coef_count = plane_modes * modes_x
    portion = lax.psum_scatter(flattened, "grp", scatter_dimension=1, tiled=True)
    squares = lax.psum(jnp.sum(portion * portion, axis=0), "slab")
    scaled = (portion * lax.rsqrt(squares / coef_count + epsilon)).astype(jnp.bfloat16)
    field_basis = lax.all_gather(scaled, "grp", axis=1, tiled=True)
    slab_modes = field_basis.shape[0] // modes_x
    basis_rows = field_basis.reshape(slab_modes, modes_x, fields)
    gamma_rows = local_rows.reshape(slab_modes, -1, modes_x)
    summed = lax.psum_scatter(
        jnp.einsum("ypk,ykf->pf", gamma_rows, basis_rows, preferred_element_type=jnp.float32),
        "slab",
        scatter_dimension=0,
        tiled=True,
    )
    return summed * (1.0 / math.sqrt(coef_count))


def solution(mesh):
    return jax.shard_map(
        body,
        mesh=mesh,
        in_specs=(
            P(("grp", "slab"), None, None),
            P(("grp", "slab"), None, None),
            P(("grp", "slab")),
            P(("grp", "slab")),
            P("grp", None),
        ),
        out_specs=P(("grp", "slab"), None),
        check_vma=False,
    )
```

profile of v0, /device:TPU:32, one launch (start us, length us, event | category | flops | bytes accessed | tf_op | source)
XLA Modules:
  0.0 870.3 jit_solution(2158189540496240035)
XLA Ops:
  6.5 0.0 copy-start
  6.5 0.0 reduce-scatter.3.cloned.1.call-start
  6.6 0.8 compare_select_fusion.1
  7.4 0.7 compare_select_fusion
  8.1 0.0 copy-done
  8.1 7.2 gather_fusion
  15.3 9.4 %gather_fusion.1 = bf16[32,64,4096]{2,1,0:T(8,128)(2,1)} fusion(bf16[8,64,4096]{2,1,0:T(8,128)(2,1)} %param.6, s32[1024]{0:T(1024)S(1)} %pad_clamp_fusion), kind=kCustom, calls=%fused_computation.1 | custom fusion | bytes 33554560 | tf_op jit(solution)/shard_map/gather | solution.py:55
  24.7 23.4 %convert_bitcast_fusion = bf16[32,64,4096]{2,1,0:T(8,128)(2,1)} fusion(bf16[32,64,4096]{2,1,0:T(8,128)(2,1)} %gather_fusion.1, bf16[32,64,4096]{2,1,0:T(8,128)(2,1)} %gather_fusion, f32[64]{0:T(128)S(1)} %get-tuple-element.5, f32[64]{0:T(128)S(1)} %fusion.20, f32[64]{0:T(128)S(1)} %get-tuple-element.6, pred[64]{0:T(512)(128)(4,1)S(1)} %compare_or_fusion), kind=kOutput, calls=%fused_computation.6 | convolution fusion | flops 1115705344 | bytes 50332480 | tf_op jit(solution)/shard_map/pxs,xk->pks/dot_general | solution.py:42
  48.2 46.0 %reshape.261 = bf16[2048,64,64]{2,1,0:T(8,128)(2,1)} reshape(bf16[32,64,4096]{2,1,0:T(8,128)(2,1)} %convert_bitcast_fusion) | data formatting | bytes 33554432 | tf_op jit(solution)/shard_map/reshape | solution.py:45
  94.2 0.1 broadcast_add_fusion
  94.2 0.1 add.182
  94.3 0.2 divide_sqrt_fusion
  94.5 0.2 copy.19
  94.7 6.8 mul.166
  101.5 14.8 %mul.167 = f32[32,32,2048]{2,1,0:T(8,128)} reshape(f32[1024,32,64]{2,1,0:T(8,128)} %mul.166) | data formatting | bytes 16777216 | tf_op jit(solution)/shard_map/mul | solution.py:50
  116.3 0.0 copy-start.2
  116.3 75.2 %convert_bitcast_fusion.1 = bf16[32,64,2048]{2,0,1:T(8,128)(2,1)} fusion(bf16[2048,64,64]{2,1,0:T(8,128)(2,1)} %reshape.261, f32[32]{0:T(128)S(1)} %or_select_fusion.1, f32[32]{0:T(128)S(1)} %fusion.21, f32[64]{0:T(128)S(1)} %get-tuple-element.6, pred[32]{0:T(512)(128)(4,1)S(1)} %compare_or_fusion.1), kind=kOutput, calls=%fused_computation.11 | convolution fusion | flops 541075456 | bytes 25166368 | tf_op jit(solution)/shard_map/ayz,zc->cya/dot_general | solution.py:46
  191.5 0.0 copy-done.2
  191.5 18.1 %fusion.3 = bf16[32,32,2048]{2,0,1:T(8,128)(2,1)S(1)} fusion(f32[32,32,2048]{2,1,0:T(8,128)S(1)} %copy-done.2, bf16[32,64,2048]{2,0,1:T(8,128)(2,1)} %convert_bitcast_fusion.1, f32[32]{0:T(128)S(1)} %or_select_fusion.1, f32[32]{0:T(128)S(1)} %fusion.21, f32[64]{0:T(128)S(1)} %get-tuple-element.6, pred[32]{0:T(512)(128)(4,1)S(1)} %compare_or_fusion.1), kind=kOutput, calls=%fused_computation.8 | convolution fusion | flops 272640000 | bytes 20972064 | tf_op jit(solution)/shard_map/cya,yb->bca/dot_general | solution.py:49
  209.7 2.3 copy.21
  212.0 111.3 %all_to_all.15 = bf16[32,32,2048]{2,1,0:T(8,128)(2,1)S(1)} all-to-all(bf16[32,32,2048]{2,1,0:T(8,128)(2,1)S(1)} %copy.21), channel_id=1, replica_groups=mesh['grp'=8,'slab'=32] {'slab'}, dimensions={0} | all-to-all | bytes 8388608 | tf_op jit(solution)/shard_map/all_to_all | solution.py:60
  323.3 4.3 copy.22
  327.5 12.9 %reshape_squeeze.4 = bf16[32,1024,64]{2,1,0:T(8,128)(2,1)} reshape(bf16[1,32,32,2048]{3,2,1,0:T(8,128)(2,1)} %copy.22) | data formatting | bytes 8388608 | tf_op jit(solution)/shard_map/reshape;squeeze | solution.py:73
  340.4 0.0 copy-start.3
  340.4 8.7 copy.23
  349.1 0.0 copy-done.3
  349.1 8.9 %fusion.27 = f32[2048,1024]{1,0:T(8,128)} fusion(bf16[2048,1024]{1,0:T(8,128)(2,1)} %bitcast.27, bf16[1024,1024]{1,0:T(8,128)(2,1)S(1)} %copy-done.3), kind=kOutput, calls=%fused_computation.56 | convolution fusion | flops 4294967296 | bytes 14680064 | tf_op jit(solution)/shard_map/npk,pf->nkf/dot_general | solution.py:63
  358.0 0.0 reduce-scatter.3.cloned.1.call-update
  358.0 0.0 all-gather.2.cloned.1.call-start
  358.1 86.6 %reduce-scatter.3.cloned.1.call-done = f32[2048,128]{1,0:T(8,128)} async-done(((f32[2048,1024]{1,0:T(8,128)}), f32[2048,128]{1,0:T(8,128)}) %reduce-scatter.3.cloned.1.call-update) | async-done | bytes 1048592 | tf_op jit(solution)/shard_map/reduce_scatter | solution.py:67
  444.6 1.5 multiply_reduce_fusion
  446.1 118.9 %psum.7 = f32[128]{0:T(128)S(1)} all-reduce(f32[128]{0:T(128)S(1)} %multiply_reduce_fusion), channel_id=1, replica_groups=mesh['grp'=8,'slab'=32] {'slab'}, use_global_device_ids=true, to_apply=%region_2.3 | all-reduce | flops 128 | bytes 1024 | tf_op jit(solution)/shard_map/psum | solution.py:68
  565.0 2.1 multiply_convert_fusion.4
  567.1 0.0 all-gather.2.cloned.1.call-update
  567.1 0.0 reduce-scatter.5.cloned.1.call-start
  567.2 46.7 %all-gather.2.cloned.1.call-done = bf16[2048,1024]{1,0:T(8,128)(2,1)} async-done(((bf16[2048,128]{1,0:T(8,128)(2,1)}), bf16[2048,1024]{1,0:T(8,128)(2,1)}) %all-gather.2.cloned.1.call-update) | async-done | bytes 4194320 | tf_op jit(solution)/shard_map/all_gather | solution.py:70
  613.8 0.0 copy-start.1
  613.8 9.7 %convolution_bitcast_fusion = f32[1024,1024]{1,0:T(8,128)} fusion(bf16[32,1024,64]{2,1,0:T(8,128)(2,1)} %reshape_squeeze.4, bf16[32,64,1024]{2,1,0:T(8,128)(2,1)} %bitcast.28), kind=kOutput, calls=%fused_computation.12 | convolution fusion | flops 4294967296 | bytes 12582912 | tf_op jit(solution)/shard_map/ypk,ykf->pf/dot_general | solution.py:75
  623.5 0.0 reduce-scatter.5.cloned.1.call-update
  623.5 238.5 %reduce-scatter.5.cloned.1.call-done = f32[32,1024]{1,0:T(8,128)} async-done(((f32[1024,1024]{1,0:T(8,128)}), f32[32,1024]{1,0:T(8,128)}) %reduce-scatter.5.cloned.1.call-update) | async-done | bytes 131088 | tf_op jit(solution)/shard_map/reduce_scatter | solution.py:74
  862.0 1.6 broadcast_multiply_fusion
  863.6 0.0 copy-done.1
  (11 shorter events, 0.1 us)
Async XLA Ops:
  6.5 1.6 copy-start
  6.5 438.1 %reduce-scatter.3.cloned.1.call-start = ((), (), s32[]{:S(2)}) async-start(), calls=%async_computation.3 | async-start | bytes 9437184 | tf_op jit(solution)/shard_map/reduce_scatter | solution.py:67
  116.3 75.2 %copy-start.2 = (f32[32,32,2048]{2,1,0:T(8,128)S(1)}, f32[32,32,2048]{2,1,0:T(8,128)}, u32[]{:S(2)}) copy-start(f32[32,32,2048]{2,1,0:T(8,128)} %mul.167) | copy-start | bytes 25165828
  340.4 8.7 copy-start.3
  358.0 255.8 %all-gather.2.cloned.1.call-start = ((), (), s32[]{:S(2)}) async-start(), calls=%async_computation.4 | async-start | bytes 4718592 | tf_op jit(solution)/shard_map/all_gather | solution.py:70
  567.1 294.9 %reduce-scatter.5.cloned.1.call-start = ((), (), s32[]{:S(2)}) async-start(), calls=%async_computation.5 | async-start | bytes 4325376 | tf_op jit(solution)/shard_map/reduce_scatter | solution.py:74
  613.8 249.8 %copy-start.1 = (bf16[4,64,4096]{2,1,0:T(8,128)(2,1)S(1)}, bf16[4,64,4096]{2,1,0:T(8,128)(2,1)}, u32[]{:S(2)}) copy-start(bf16[4,64,4096]{2,1,0:T(8,128)(2,1)} %param.5) | copy-start | bytes 6291460
Sparse Core Ops, SparseCore 0:
  358.1 86.4 reduce-scatter.2
  567.2 46.5 all-gather.1
  623.7 238.3 reduce-scatter.4
where the time goes:
time: 878 us; the launch traced here: 870 us
  waiting for transfers between devices  372 us (42%)
  blocking collectives  230 us (26%)
  matrix products  135 us (15%)
  local copies, waits for them, and re-layouts  113 us (13%)
  between operations  13.4 us (2%)
    reduce_scatter x1, waiting for transfers between devices, body(): lax.psum_scatter(jnp.einsum('ypk,ykf->pf', gamma_rows, basis_rows, prefer...  238 us
    psum x1, blocking collectives, body(): squares = lax.psum(jnp.sum(portion * portion, axis=0), 'slab')  119 us
    all_to_all x1, blocking collectives, body(): lax.all_to_all(parcel, 'slab', split_axis=0, concat_axis=2, tiled=True)  111 us
    reduce_scatter x1, waiting for transfers between devices, body(): lax.psum_scatter(flattened, 'grp', scatter_dimension=1, tiled=True)  86.6 us
    dot_general x1, matrix products, pair_coefficients(): jnp.einsum('ayz,zc->cya', planes, basis_plane, preferred_element_type=jnp...  75.2 us
    all_gather x1, waiting for transfers between devices, body(): field_basis = lax.all_gather(scaled, 'grp', axis=1, tiled=True)  46.7 us
    reshape x1, local copies, waits for them, and re-layouts, pair_coefficients(): planes = along_x.reshape(pairs_dev * grid_size, grid_size, grid_size)  46 us
    dot_general x1, matrix products, pair_coefficients(): jnp.einsum('pxs,xk->pks', density, basis_x, preferred_element_type=jnp.fl...  23.4 us
  transfers between devices with their start and end apart: 3, of which 3 were waited for; matrix products, arithmetic and copies ran while one was open for 0% of the time, Pallas kernels for 0%

commit v1 on v0

--- a/solution.py
+++ b/solution.py
@@ -67,7 +67,15 @@
     portion = lax.psum_scatter(flattened, "grp", scatter_dimension=1, tiled=True)
     squares = lax.psum(jnp.sum(portion * portion, axis=0), "slab")
     scaled = (portion * lax.rsqrt(squares / coef_count + epsilon)).astype(jnp.bfloat16)
-    field_basis = lax.all_gather(scaled, "grp", axis=1, tiled=True)
+    field_basis = jnp.concatenate(
+        lax.all_to_all(
+            jnp.stack([scaled] * lax.axis_size("grp"), axis=0),
+            axis_name="grp",
+            split_axis=0,
+            concat_axis=0,
+        ),
+        axis=1,
+    )
     slab_modes = field_basis.shape[0] // modes_x
     basis_rows = field_basis.reshape(slab_modes, modes_x, fields)
     gamma_rows = local_rows.reshape(slab_modes, -1, modes_x)

time: 878 us -> 951 us (1.083)
  blocking collectives: 230 us -> 325 us
  waiting for transfers between devices: 372 us -> 320 us
  local copies, waits for them, and re-layouts: 113 us -> 134 us
    all_to_all x0 -> x1, blocking collectives: none -> 95 us  [body(): lax.all_to_all(jnp.stack([scaled] * lax.axis_size('grp'), axis=0), axis_n...]
    all_gather x1 -> x0, waiting for transfers between devices: 46.7 us -> none  [body(): field_basis = lax.all_gather(scaled, 'grp', axis=1, tiled=True)]
    reshape x0 -> x1, local copies, waits for them, and re-layouts: none -> 13.2 us  [body(): jnp.concatenate(lax.all_to_all(jnp.stack([scaled] * lax.axis_size('grp'),...]
  transfers between devices with their start and end apart: 3 -> 2, of which waited for: 3 -> 2; matrix products, arithmetic and copies ran while one was open for 0% -> 0% of each run, Pallas kernels for 0% -> 0%
where the time goes in v1:
time: 951 us; the launch traced here: 943 us
  blocking collectives  325 us (34%)
  waiting for transfers between devices  320 us (34%)
  matrix products  144 us (15%)
  local copies, waits for them, and re-layouts  134 us (14%)
  between operations  14 us (1%)
    reduce_scatter x1, waiting for transfers between devices, body(): lax.psum_scatter(jnp.einsum('ypk,ykf->pf', gamma_rows, basis_rows, prefer...  233 us
    psum x1, blocking collectives, body(): squares = lax.psum(jnp.sum(portion * portion, axis=0), 'slab')  119 us
    all_to_all x1, blocking collectives, body(): lax.all_to_all(parcel, 'slab', split_axis=0, concat_axis=2, tiled=True)  111 us
    all_to_all x1, blocking collectives, body(): lax.all_to_all(jnp.stack([scaled] * lax.axis_size('grp'), axis=0), axis_n...  95 us
    reduce_scatter x1, waiting for transfers between devices, body(): lax.psum_scatter(flattened, 'grp', scatter_dimension=1, tiled=True)  86.6 us
    dot_general x1, matrix products, pair_coefficients(): jnp.einsum('ayz,zc->cya', planes, basis_plane, preferred_element_type=jnp...  83.4 us
    reshape x1, local copies, waits for them, and re-layouts, pair_coefficients(): planes = along_x.reshape(pairs_dev * grid_size, grid_size, grid_size)  46 us
    dot_general x1, matrix products, pair_coefficients(): jnp.einsum('pxs,xk->pks', density, basis_x, preferred_element_type=jnp.fl...  23.4 us
  transfers between devices with their start and end apart: 2, of which 2 were waited for; matrix products, arithmetic and copies ran while one was open for 0% of the time, Pallas kernels for 0%

profile of v1, /device:TPU:32, one launch (start us, length us, event | category | flops | bytes accessed | tf_op | source)
XLA Modules:
  0.0 942.6 jit_solution(14064590833864545182)
XLA Ops:
  6.5 0.0 copy-start
  6.5 0.0 reduce-scatter.3.cloned.1.call-start
  6.6 0.8 compare_select_fusion.1
  7.4 0.7 compare_select_fusion
  8.1 0.0 copy-done
  8.1 7.2 gather_fusion
  15.3 9.4 gather_fusion.1
  24.7 23.4 %convert_bitcast_fusion = bf16[32,64,4096]{2,1,0:T(8,128)(2,1)} fusion(bf16[32,64,4096]{2,1,0:T(8,128)(2,1)} %gather_fusion.1, bf16[32,64,4096]{2,1,0:T(8,128)(2,1)} %gather_fusion, f32[64]{0:T(128)S(1)} %get-tuple-element.5, f32[64]{0:T(128)S(1)} %fusion.20, f32[64]{0:T(128)S(1)} %get-tuple-element.6, pred[64]{0:T(512)(128)(4,1)S(1)} %compare_or_fusion), kind=kOutput, calls=%fused_computation.6 | convolution fusion | flops 1115705344 | bytes 50332480 | tf_op jit(solution)/shard_map/pxs,xk->pks/dot_general | solution.py:42
  48.1 46.0 %reshape.263 = bf16[2048,64,64]{2,1,0:T(8,128)(2,1)} reshape(bf16[32,64,4096]{2,1,0:T(8,128)(2,1)} %convert_bitcast_fusion) | data formatting | bytes 33554432 | tf_op jit(solution)/shard_map/reshape | solution.py:45
  94.1 0.1 broadcast_add_fusion
  94.2 0.1 add.182
  94.3 0.2 divide_sqrt_fusion
  94.5 0.2 copy.20
  94.7 6.8 mul.166
  101.4 14.8 %mul.167 = f32[32,32,2048]{2,1,0:T(8,128)} reshape(f32[1024,32,64]{2,1,0:T(8,128)} %mul.166) | data formatting | bytes 16777216 | tf_op jit(solution)/shard_map/mul | solution.py:50
  116.2 0.0 copy-start.2
  116.2 83.4 %convert_bitcast_fusion.1 = bf16[32,64,2048]{2,0,1:T(8,128)(2,1)} fusion(bf16[2048,64,64]{2,1,0:T(8,128)(2,1)} %reshape.263, f32[32]{0:T(128)S(1)} %or_select_fusion.1, f32[32]{0:T(128)S(1)} %fusion.21, f32[64]{0:T(128)S(1)} %get-tuple-element.6, pred[32]{0:T(512)(128)(4,1)S(1)} %compare_or_fusion.1), kind=kOutput, calls=%fused_computation.11 | convolution fusion | flops 541075456 | bytes 25166368 | tf_op jit(solution)/shard_map/ayz,zc->cya/dot_general | solution.py:46
  199.7 0.0 copy-done.2
  199.7 18.2 %fusion.3 = bf16[32,32,2048]{2,0,1:T(8,128)(2,1)S(1)} fusion(f32[32,32,2048]{2,1,0:T(8,128)S(1)} %copy-done.2, bf16[32,64,2048]{2,0,1:T(8,128)(2,1)} %convert_bitcast_fusion.1, f32[32]{0:T(128)S(1)} %or_select_fusion.1, f32[32]{0:T(128)S(1)} %fusion.21, f32[64]{0:T(128)S(1)} %get-tuple-element.6, pred[32]{0:T(512)(128)(4,1)S(1)} %compare_or_fusion.1), kind=kOutput, calls=%fused_computation.8 | convolution fusion | flops 272640000 | bytes 20972064 | tf_op jit(solution)/shard_map/cya,yb->bca/dot_general | solution.py:49
  217.9 2.3 copy.22
  220.2 111.3 %all_to_all.20 = bf16[32,32,2048]{2,1,0:T(8,128)(2,1)S(1)} all-to-all(bf16[32,32,2048]{2,1,0:T(8,128)(2,1)S(1)} %copy.22), channel_id=1, replica_groups=mesh['grp'=8,'slab'=32] {'slab'}, dimensions={0} | all-to-all | bytes 8388608 | tf_op jit(solution)/shard_map/all_to_all | solution.py:60
  331.4 4.3 copy.23
  335.7 12.9 %reshape_squeeze.4 = bf16[32,1024,64]{2,1,0:T(8,128)(2,1)} reshape(bf16[1,32,32,2048]{3,2,1,0:T(8,128)(2,1)} %copy.23) | data formatting | bytes 8388608 | tf_op jit(solution)/shard_map/reshape;squeeze | solution.py:81
  348.6 0.0 copy-start.3
  348.6 8.7 copy.24
  357.3 0.0 copy-done.3
  357.3 8.9 fusion.27
  366.2 0.0 reduce-scatter.3.cloned.1.call-update
  366.2 0.0 reduce-scatter.5.cloned.1.call-start
  366.3 86.6 %reduce-scatter.3.cloned.1.call-done = f32[2048,128]{1,0:T(8,128)} async-done(((f32[2048,1024]{1,0:T(8,128)}), f32[2048,128]{1,0:T(8,128)}) %reduce-scatter.3.cloned.1.call-update) | async-done | bytes 1048592 | tf_op jit(solution)/shard_map/reduce_scatter | solution.py:67
  452.8 1.5 multiply_reduce_fusion
  454.3 119.1 %psum.7 = f32[128]{0:T(128)S(1)} all-reduce(f32[128]{0:T(128)S(1)} %multiply_reduce_fusion), channel_id=1, replica_groups=mesh['grp'=8,'slab'=32] {'slab'}, use_global_device_ids=true, to_apply=%region_2.3 | all-reduce | flops 128 | bytes 1024 | tf_op jit(solution)/shard_map/psum | solution.py:68
  573.4 1.3 multiply_convert_fusion.4
  574.7 0.5 stack.2
  575.3 95.0 %all_to_all.21 = bf16[8,2048,128]{2,1,0:T(8,128)(2,1)S(1)} all-to-all(bf16[8,2048,128]{2,1,0:T(8,128)(2,1)S(1)} %stack.2), channel_id=1, replica_groups=mesh['grp'=8,'slab'=32] {'grp'}, dimensions={0} | all-to-all | bytes 8388608 | tf_op jit(solution)/shard_map/all_to_all | solution.py:71
  670.3 13.2 %copy.25 = bf16[2048,8,128]{2,1,0:T(8,128)(2,1)} copy(bf16[2048,8,128]{2,0,1:T(8,128)(2,1)S(1)} %bitcast.27) | data formatting | bytes 8388608 | tf_op jit(solution)/shard_map/reshape | solution.py:70
  683.5 7.3 reshape_reshape.3
  690.8 0.0 copy-start.1
  690.8 9.7 %convolution_bitcast_fusion = f32[1024,1024]{1,0:T(8,128)} fusion(bf16[32,1024,64]{2,1,0:T(8,128)(2,1)} %reshape_squeeze.4, bf16[32,64,1024]{2,1,0:T(8,128)(2,1)} %reshape_reshape.3), kind=kOutput, calls=%fused_computation.12 | convolution fusion | flops 4294967296 | bytes 12582912 | tf_op jit(solution)/shard_map/ypk,ykf->pf/dot_general | solution.py:83
  700.5 0.0 reduce-scatter.5.cloned.1.call-update
  700.5 233.2 %reduce-scatter.5.cloned.1.call-done = f32[32,1024]{1,0:T(8,128)} async-done(((f32[1024,1024]{1,0:T(8,128)}), f32[32,1024]{1,0:T(8,128)}) %reduce-scatter.5.cloned.1.call-update) | async-done | bytes 131088 | tf_op jit(solution)/shard_map/reduce_scatter | solution.py:82
  933.7 1.6 broadcast_multiply_fusion
  935.3 0.0 copy-done.1
  (11 shorter events, 0.1 us)
Async XLA Ops:
  6.5 1.6 copy-start
  6.5 446.3 %reduce-scatter.3.cloned.1.call-start = ((), (), s32[]{:S(2)}) async-start(), calls=%async_computation.4 | async-start | bytes 9437184 | tf_op jit(solution)/shard_map/reduce_scatter | solution.py:67
  116.2 83.4 %copy-start.2 = (f32[32,32,2048]{2,1,0:T(8,128)S(1)}, f32[32,32,2048]{2,1,0:T(8,128)}, u32[]{:S(2)}) copy-start(f32[32,32,2048]{2,1,0:T(8,128)} %mul.167) | copy-start | bytes 25165828
  348.6 8.7 copy-start.3
  366.2 567.5 %reduce-scatter.5.cloned.1.call-start = ((), (), s32[]{:S(2)}) async-start(), calls=%async_computation.5 | async-start | bytes 4325376 | tf_op jit(solution)/shard_map/reduce_scatter | solution.py:82
  690.8 244.5 %copy-start.1 = (bf16[4,64,4096]{2,1,0:T(8,128)(2,1)S(1)}, bf16[4,64,4096]{2,1,0:T(8,128)(2,1)}, u32[]{:S(2)}) copy-start(bf16[4,64,4096]{2,1,0:T(8,128)(2,1)} %param.5) | copy-start | bytes 6291460
Sparse Core Ops, SparseCore 0:
  366.3 86.4 reduce-scatter.2
  700.7 232.9 reduce-scatter.4
